TPU v7x, 32 devices: a whole 2x2x4 slice. The times are simulated.
32 devices in a mesh: groups: 2 (over y), tensor: 4 (over z), dp: 4 (over x, core).
Axes of the slice: x: 2, y: 2, z: 4, core: 2. Of those that a mesh axis runs over, the one named last changes fastest.
Arguments:
- tokens: bfloat16 [256, 8192], P(('groups', 'tensor', 'dp')), parts along dimension 0, may hold values from -6 to 6
- gate_projection_matrix: bfloat16 [8192, 14336], P('dp', 'tensor'), may hold values from -0.0625 to 0.0625
- up_projection_matrix: bfloat16 [8192, 14336], P('dp', 'tensor'), may hold values from -0.0625 to 0.0625
- down_projection_matrix: bfloat16 [14336, 8192], P('tensor', 'dp'), may hold values from -0.046875 to 0.046875
- gate_adapter_inmap: bfloat16 [16384, 64], P(('groups', 'dp')), parts along dimension 0, may hold values from -0.0625 to 0.0625
- gate_adapter_outmap: bfloat16 [64, 28672], P(None, ('groups', 'tensor')), parts along dimension 1, may hold values from -0.75 to 0.75
- up_adapter_inmap: bfloat16 [16384, 64], P(('groups', 'dp')), parts along dimension 0, may hold values from -0.0625 to 0.0625
- up_adapter_outmap: bfloat16 [64, 28672], P(None, ('groups', 'tensor')), parts along dimension 1, may hold values from -0.75 to 0.75
- down_adapter_inmap: bfloat16 [28672, 64], P(('groups', 'tensor')), parts along dimension 0, may hold values from -0.046875 to 0.046875
- down_adapter_outmap: bfloat16 [64, 16384], P(None, 'groups'), parts along dimension 1, may hold values from -0.75 to 0.75
Outputs:
- block_out: bfloat16 [256, 8192], P(('groups', 'tensor', 'dp')), parts along dimension 0
There are 2 independent parts, one for each index of `groups`. A program takes and returns all parts, laid end to end along the dimension named above; an argument that names none is the same for every part. Nothing has to cross between parts.
All inputs are finite; a program needn't handle non-finite values.
Results may differ from a plain program's by a relative error of at most 0.0053.
Values may be sent and summed in bfloat16 or wider, within the bound.
A program may use at most 256 MiB of HBM per device.

v0:
```python
import jax
import jax.numpy as jnp
from jax import lax
from jax.sharding import PartitionSpec as P

adapter_scale_factor = 0.5


def body(
    tokens,
    gate_projection_matrix,
    up_projection_matrix,
    down_projection_matrix,
    gate_adapter_inmap,
    gate_adapter_outmap,
    up_adapter_inmap,
    up_adapter_outmap,
    down_adapter_inmap,
    down_adapter_outmap,
):
    tok_dev = tokens.shape[0]
    n_tensor = lax.axis_size("tensor")
    n_dp = lax.axis_size("dp")
    hidden_unit_count = gate_projection_matrix.shape[1]
    adapter_rank_size = gate_adapter_inmap.shape[1]
    columns = lax.all_to_all(tokens, "dp", split_axis=1, concat_axis=0, tiled=True)
    stacked_lowrank = jnp.concatenate(
        [gate_projection_matrix, up_projection_matrix, gate_adapter_inmap, up_adapter_inmap], axis=1
    )
    partial_all = jnp.dot(
        lax.all_gather(columns, "tensor", axis=0, tiled=True),
        stacked_lowrank,
        preferred_element_type=jnp.float32,
    )
    partial_all = partial_all.reshape(n_tensor, n_dp, tok_dev, partial_all.shape[1])
    summed_lowrank = lax.psum_scatter(partial_all, "dp", scatter_dimension=1, tiled=True)
    summed_lowrank = summed_lowrank.reshape(n_tensor * tok_dev, summed_lowrank.shape[3])
    gate_dense_part = summed_lowrank[:, :hidden_unit_count]
    up_dense_part = summed_lowrank[:, hidden_unit_count : 2 * hidden_unit_count]
    gate_lowrank_part = summed_lowrank[
        :, 2 * hidden_unit_count : 2 * hidden_unit_count + adapter_rank_size
    ].astype(jnp.bfloat16)
    up_lowrank_part = summed_lowrank[:, 2 * hidden_unit_count + adapter_rank_size :].astype(
        jnp.bfloat16
    )
    gate_activated = gate_dense_part + adapter_scale_factor * jnp.dot(
        gate_lowrank_part, gate_adapter_outmap, preferred_element_type=jnp.float32
    )
    up_projected_value = up_dense_part + adapter_scale_factor * jnp.dot(
        up_lowrank_part, up_adapter_outmap, preferred_element_type=jnp.float32
    )
    hidden_product = (jax.nn.silu(gate_activated) * up_projected_value).astype(jnp.bfloat16)
    down_outmap_single = down_adapter_outmap.astype(jnp.float32)
    lowrank_term_list = jnp.dot(
        hidden_product, down_adapter_inmap, preferred_element_type=jnp.float32
    )
    owned_lowrank_part = lax.psum_scatter(
        lowrank_term_list, "tensor", scatter_dimension=0, tiled=True
    )
    term = jnp.dot(
        hidden_product,
        lax.all_gather(down_projection_matrix, "dp", axis=1, tiled=True),
        preferred_element_type=jnp.float32,
    )
    block_result_rows = lax.psum_scatter(term, "tensor", scatter_dimension=0, tiled=True)
    block_result_rows = block_result_rows + adapter_scale_factor * jnp.dot(
        owned_lowrank_part, down_outmap_single, precision=lax.Precision.HIGHEST
    )
    return block_result_rows.astype(jnp.bfloat16)


def solution(mesh):
    placed = (
        P(("groups", "tensor", "dp"), None),
        P("dp", "tensor"),
        P("dp", "tensor"),
        P("tensor", "dp"),
        P(("groups", "dp"), None),
        P(None, ("groups", "tensor")),
        P(("groups", "dp"), None),
        P(None, ("groups", "tensor")),
        P(("groups", "tensor"), None),
        P(None, "groups"),
    )
    return jax.shard_map(
        body,
        mesh=mesh,
        in_specs=placed,
        out_specs=P(("groups", "tensor", "dp"), None),
        check_vma=False,
    )
```

profile of v0, /device:TPU:0, one launch (start us, length us, event | category | flops | bytes accessed | tf_op | source)
XLA Modules:
  0.0 576.1 jit_solution(376535880790217102)
XLA Ops:
  6.5 0.0 copy-start
  6.5 4.4 all-to-all-start
  10.9 0.0 all-reduce.4.cloned.1.call-start
  10.9 1.2 copy.13
  12.1 1.2 copy.14
  13.4 44.4 %concatenate.3 = bf16[2048,7296]{1,0:T(8,128)(2,1)} concatenate(bf16[2048,3584]{1,0:T(8,128)(2,1)} %param.11, bf16[2048,3584]{1,0:T(8,128)(2,1)} %param.12, bf16[2048,64]{1,0:T(8,128)(2,1)S(1)} %copy.13, bf16[2048,64]{1,0:T(8,128)(2,1)S(1)} %copy.14), dimensions={1} | concatenate | bytes 59768832 | tf_op jit(solution)/shard_map/concatenate | solution.py:27
  57.7 0.0 copy-start.5
  57.8 0.0 copy-start.2
  57.8 0.0 copy-start.3
  57.8 0.0 all-to-all-done
  57.8 17.1 %all_gather.6 = bf16[128,2048]{1,0:T(8,128)(2,1)S(1)} all-gather(bf16[32,2048]{1,0:T(8,128)(2,1)S(1)} %bitcast.24), channel_id=1, replica_groups=mesh['groups'=2,'tensor'=4,'dp'=4] {'tensor'}, dimensions={0}, use_global_device_ids=true | all-gather | bytes 655360 | tf_op jit(solution)/shard_map/all_gather | solution.py:31
  74.9 15.4 %fusion.13 = f32[7296,128]{0,1:T(8,128)} fusion(bf16[128,2048]{1,0:T(8,128)(2,1)S(1)} %all_gather.6, bf16[2048,7296]{1,0:T(8,128)(2,1)} %concatenate.3), kind=kOutput, calls=%fused_computation.17 | convolution fusion | flops 3825205248 | bytes 34144256 | tf_op jit(solution)/shard_map/dot_general | solution.py:30
  90.3 0.0 all-reduce.4.cloned.1.call-update
  90.3 0.0 all-gather.2.cloned.1.call-start
  90.4 0.7 all-gather.2.cloned.1.call-update
  91.1 0.0 reduce-scatter.3.cloned.1.call-start
  91.2 0.0 copy-done.5
  91.2 0.6 dynamic-slice
  91.7 78.5 %all-reduce.4.cloned.1.call-done = f32[4,4,8,7296]{3,2,1,0:T(8,128)} async-done(((f32[4,4,8,7296]{3,2,1,0:T(8,128)}), f32[4,4,8,7296]{3,2,1,0:T(8,128)}) %all-reduce.4.cloned.1.call-update) | async-done | bytes 3735568
  170.2 1.9 fusion.10
  172.2 0.0 copy-done.2
  172.2 0.2 fusion.4
  172.4 0.0 copy-done.3
  172.4 0.3 fusion.5
  172.7 0.0 copy-start.4
  172.7 0.0 copy-start.1
  172.7 345.2 %all-gather.2.cloned.1.call-done = bf16[3584,8192]{1,0:T(8,128)(2,1)} async-done(((bf16[3584,2048]{1,0:T(8,128)(2,1)}), bf16[3584,8192]{1,0:T(8,128)(2,1)}) %all-gather.2.cloned.1.call-update) | async-done | bytes 58720272 | tf_op jit(solution)/shard_map/all_gather | solution.py:62
  518.0 21.6 %fusion.11 = f32[32,8192]{1,0:T(8,128)} fusion(bf16[32,3584]{1,0:T(8,128)(2,1)S(1)} %fusion.5, bf16[3584,8192]{1,0:T(8,128)(2,1)} %all-gather.2.cloned.1.call-done), kind=kOutput, calls=%fused_computation.15 | convolution fusion | flops 1879048192 | bytes 59998208 | tf_op jit(solution)/shard_map/dot_general | solution.py:60
  539.6 0.0 reduce-scatter.3.cloned.1.call-update
  539.6 0.0 copy-done.4
  539.6 0.6 dynamic-slice.2
  540.9 0.0 copy-done.1
  540.9 0.2 fusion.12
  541.1 19.7 %all-reduce.1 = f32[32,64]{1,0:T(8,128)S(1)} all-reduce(f32[32,64]{1,0:T(8,128)S(1)} %fusion.12), channel_id=4, replica_groups=mesh['groups'=2,'tensor'=4,'dp'=4] {'tensor'}, use_global_device_ids=true, to_apply=%region_2.3.clone | all-reduce | flops 2048 | bytes 16384
  560.9 6.6 %reduce-scatter.3.cloned.1.call-done = f32[8,8192]{1,0:T(8,128)} async-done(((f32[32,8192]{1,0:T(8,128)}), f32[8,8192]{1,0:T(8,128)}) %reduce-scatter.3.cloned.1.call-update) | async-done | bytes 262160 | tf_op jit(solution)/shard_map/reduce_scatter | solution.py:65
  567.4 0.0 copy-done
  567.4 2.1 fusion.1
Async XLA Ops:
  6.5 560.9 %copy-start = (bf16[64,8192]{1,0:T(8,128)(2,1)S(1)}, bf16[64,8192]{1,0:T(8,128)(2,1)}, u32[]{:S(2)}) copy-start(bf16[64,8192]{1,0:T(8,128)(2,1)} %param.19) | copy-start | bytes 3145732
  6.5 51.2 %all-to-all-start = ((bf16[8,4,2048]{2,0,1:T(8,128)(2,1)}), bf16[8,4,2048]{2,0,1:T(8,128)(2,1)S(1)}, u32[]{:S(2)}, u32[]{:S(2)}) async-start(bf16[8,4,2048]{2,0,1:T(8,128)(2,1)} %bitcast.25), calls=%async_computation | async-start | bytes 262144 | tf_op jit(solution)/shard_map/all_to_all | solution.py:26
  10.9 159.3 %all-reduce.4.cloned.1.call-start = ((), (), s32[]{:S(2)}) async-start(), calls=%async_computation.4 | async-start | bytes 7471104
  57.7 33.4 %copy-start.5 = (u32[32]{0:T(128)S(1)}, u32[32]{0:T(128)}, u32[]{:S(2)}) copy-start(u32[32]{0:T(128)} %constant.9) | copy-start | bytes 388
  57.8 114.4 %copy-start.2 = (bf16[64,3584]{1,0:T(8,128)(2,1)S(1)}, bf16[64,3584]{1,0:T(8,128)(2,1)}, u32[]{:S(2)}) copy-start(bf16[64,3584]{1,0:T(8,128)(2,1)} %param.15) | copy-start | bytes 1376260
  57.8 114.6 %copy-start.3 = (bf16[64,3584]{1,0:T(8,128)(2,1)S(1)}, bf16[64,3584]{1,0:T(8,128)(2,1)}, u32[]{:S(2)}) copy-start(bf16[64,3584]{1,0:T(8,128)(2,1)} %param.17) | copy-start | bytes 1376260
  90.3 427.6 %all-gather.2.cloned.1.call-start = ((), (), s32[]{:S(2)}) async-start(), calls=%async_computation.2 | async-start | bytes 73400320 | tf_op jit(solution)/shard_map/all_gather | solution.py:62
  91.1 476.3 %reduce-scatter.3.cloned.1.call-start = ((), (), s32[]{:S(2)}) async-start(), calls=%async_computation.3 | async-start | bytes 1310720 | tf_op jit(solution)/shard_map/reduce_scatter | solution.py:65
  172.7 366.9 %copy-start.4 = (u32[32]{0:T(128)S(1)}, u32[32]{0:T(128)}, u32[]{:S(2)}) copy-start(u32[32]{0:T(128)} %constant.13) | copy-start | bytes 388
  172.7 368.2 %copy-start.1 = (bf16[3584,64]{0,1:T(8,128)(2,1)S(1)}, bf16[3584,64]{0,1:T(8,128)(2,1)}, u32[]{:S(2)}) copy-start(bf16[3584,64]{0,1:T(8,128)(2,1)} %param.18) | copy-start | bytes 1376260
Sparse Core Ops, SparseCore 0:
  90.5 79.7 all-reduce.3
  171.8 346.1 all-gather.1
  539.8 27.6 reduce-scatter.2
where the time goes:
time: 578 us; the launch traced here: 576 us
  waiting for transfers between devices  431 us (75%)
  local copies, waits for them, and re-layouts  48 us (8%)
  matrix products  39.9 us (7%)
  blocking collectives  36.9 us (6%)
  between operations  13.9 us (2%)
    all_gather x1, waiting for transfers between devices, body(): lax.all_gather(down_projection_matrix, 'dp', axis=1, tiled=True)  345 us
    unnamed x4, waiting for transfers between devices  79.2 us
    concatenate x1, local copies, waits for them, and re-layouts, body(): jnp.concatenate([gate_projection_matrix, up_projection_matrix, gate_adapt...  44.4 us
    dot_general x1, matrix products, body(): jnp.dot(hidden_product, lax.all_gather(down_projection_matrix, 'dp', axis...  21.6 us
    unnamed x1, blocking collectives  19.7 us
    all_gather x1, blocking collectives, body(): lax.all_gather(columns, 'tensor', axis=0, tiled=True)  17.1 us
    dot_general x1, matrix products, body(): jnp.dot(lax.all_gather(columns, 'tensor', axis=0, tiled=True), stacked_lo...  15.4 us
  transfers between devices with their start and end apart: 4, of which 3 were waited for; matrix products, arithmetic and copies ran while one was open for 9% of the time, Pallas kernels for 0%

commit v1 on v0

--- a/solution.py
+++ b/solution.py
@@ -4,6 +4,13 @@
 from jax.sharding import PartitionSpec as P
 
 adapter_scale_factor = 0.5
+
+
+def exchange_gather(x, mesh_axis, along):
+    n_dev = lax.axis_size(mesh_axis)
+    pieces = jnp.stack([x for _ in range(n_dev)])
+    pieces = lax.all_to_all(pieces, mesh_axis, split_axis=0, concat_axis=0)
+    return jnp.concatenate(pieces, axis=along)
 
 
 def body(
@@ -59,7 +66,7 @@
     )
     term = jnp.dot(
         hidden_product,
-        lax.all_gather(down_projection_matrix, "dp", axis=1, tiled=True),
+        exchange_gather(down_projection_matrix, "dp", 1),
         preferred_element_type=jnp.float32,
     )
     block_result_rows = lax.psum_scatter(term, "tensor", scatter_dimension=0, tiled=True)

time: 578 us -> 823 us (1.42)
  waiting for transfers between devices: 431 us -> 619 us
  local copies, waits for them, and re-layouts: 48 us -> 88.4 us
  starting transfers between devices: 4.45 us -> 17.1 us
    all_to_all x0 -> x1, waiting for transfers between devices: none -> 472 us  [exchange_gather(): pieces = lax.all_to_all(pieces, mesh_axis, split_axis=0, concat_axis=0)]
    all_gather x1 -> x0, waiting for transfers between devices: 345 us -> none  [body(): lax.all_gather(down_projection_matrix, 'dp', axis=1, tiled=True)]
    unnamed x4 -> x3, waiting for transfers between devices: 79.2 us -> 140 us
    another operation x0 -> x1, local copies, waits for them, and re-layouts: none -> 23.4 us  [exchange_gather(): pieces = jnp.stack([x for _ in range(n_dev)])]
    unnamed x16 -> x21, local copies, waits for them, and re-layouts: 3.65 us -> 20.5 us
    all_to_all x0 -> x1, starting transfers between devices: none -> 12.6 us  [exchange_gather(): pieces = lax.all_to_all(pieces, mesh_axis, split_axis=0, concat_axis=0)]
  transfers between devices with their start and end apart: 4 -> 4, of which waited for: 3 -> 3; matrix products, arithmetic and copies ran while one was open for 9% -> 10% of each run, Pallas kernels for 0% -> 0%
where the time goes in v1:
time: 823 us; the launch traced here: 821 us
  waiting for transfers between devices  619 us (75%)
  local copies, waits for them, and re-layouts  88.4 us (11%)
  matrix products  43.2 us (5%)
  blocking collectives  37.4 us (5%)
  starting transfers between devices  17.1 us (2%)
  between operations  14.2 us (2%)
    all_to_all x1, waiting for transfers between devices, exchange_gather(): pieces = lax.all_to_all(pieces, mesh_axis, split_axis=0, concat_axis=0)  472 us
    unnamed x3, waiting for transfers between devices  140 us
    concatenate x1, local copies, waits for them, and re-layouts, body(): jnp.concatenate([gate_projection_matrix, up_projection_matrix, gate_adapt...  44.5 us
    dot_general x1, matrix products, body(): jnp.dot(hidden_product, exchange_gather(down_projection_matrix, 'dp', 1),...  25 us
    another operation x1, local copies, waits for them, and re-layouts, exchange_gather(): pieces = jnp.stack([x for _ in range(n_dev)])  23.4 us
    unnamed x21, local copies, waits for them, and re-layouts  20.5 us
    unnamed x1, blocking collectives  20.3 us
    all_gather x1, blocking collectives, body(): lax.all_gather(columns, 'tensor', axis=0, tiled=True)  17.1 us
  transfers between devices with their start and end apart: 4, of which 3 were waited for; matrix products, arithmetic and copies ran while one was open for 10% of the time, Pallas kernels for 0%

profile of v1, /device:TPU:0, one launch (start us, length us, event | category | flops | bytes accessed | tf_op | source)
XLA Modules:
  0.0 820.8 jit_solution(10929038281734506860)
XLA Ops:
  6.5 0.0 copy-start
  6.5 4.4 all-to-all-start
  10.9 18.8 %copy.18 = bf16[3584,2048]{0,1:T(8,128)(2,1)} copy(bf16[3584,2048]{1,0:T(8,128)(2,1)} %param.13) | data formatting | bytes 29360128 | tf_op args[3]
  29.7 0.0 all-to-all-done
  29.7 23.4 %stack.2 = bf16[4,3584,2048]{1,2,0:T(8,128)(2,1)} broadcast(bf16[3584,2048]{0,1:T(8,128)(2,1)} %copy.18), dimensions={1,2} | broadcast | bytes 73400320 | tf_op jit(solution)/shard_map/stack | solution.py:11
  53.1 0.0 copy-start.3
  53.1 0.0 copy-start.4
  53.1 12.6 %all-to-all-start.1 = ((bf16[4,3584,2048]{1,2,0:T(8,128)(2,1)}), bf16[4,3584,2048]{1,2,0:T(8,128)(2,1)}, u32[]{:S(2)}, u32[]{:S(2)}) async-start(bf16[4,3584,2048]{1,2,0:T(8,128)(2,1)} %stack.2), calls=%async_computation.1 | async-start | bytes 117440512 | tf_op jit(solution)/shard_map/all_to_all | solution.py:12
  65.7 0.0 all-reduce.4.cloned.1.call-start
  65.7 0.0 copy-done.3
  65.8 0.3 copy.16
  66.0 0.0 copy-done.4
  66.0 0.3 copy.17
  66.3 44.5 %concatenate.3 = bf16[2048,7296]{1,0:T(8,128)(2,1)} concatenate(bf16[2048,3584]{1,0:T(8,128)(2,1)} %param.11, bf16[2048,3584]{1,0:T(8,128)(2,1)} %param.12, bf16[2048,64]{1,0:T(8,128)(2,1)S(1)} %copy.16, bf16[2048,64]{1,0:T(8,128)(2,1)S(1)} %copy.17), dimensions={1} | concatenate | bytes 59768832 | tf_op jit(solution)/shard_map/concatenate | solution.py:34
  110.8 0.0 copy-start.7
  110.8 0.0 copy-start.2
  110.8 0.0 copy-start.5
  110.8 17.1 %all_gather.3 = bf16[128,2048]{1,0:T(8,128)(2,1)S(1)} all-gather(bf16[32,2048]{1,0:T(8,128)(2,1)S(1)} %bitcast.27), channel_id=1, replica_groups=mesh['groups'=2,'tensor'=4,'dp'=4] {'tensor'}, dimensions={0}, use_global_device_ids=true | all-gather | bytes 655360 | tf_op jit(solution)/shard_map/all_gather | solution.py:38
  127.9 15.4 %fusion.13 = f32[7296,128]{0,1:T(8,128)} fusion(bf16[128,2048]{1,0:T(8,128)(2,1)S(1)} %all_gather.3, bf16[2048,7296]{1,0:T(8,128)(2,1)} %concatenate.3), kind=kOutput, calls=%fused_computation.17 | convolution fusion | flops 3825205248 | bytes 34144256 | tf_op jit(solution)/shard_map/dot_general | solution.py:37
  143.3 0.0 all-reduce.4.cloned.1.call-update
  143.3 0.0 reduce-scatter.3.cloned.1.call-start
  143.4 0.0 copy-done.7
  143.4 0.6 dynamic-slice
  144.0 139.7 %all-reduce.4.cloned.1.call-done = f32[4,4,8,7296]{3,2,1,0:T(8,128)} async-done(((f32[4,4,8,7296]{3,2,1,0:T(8,128)}), f32[4,4,8,7296]{3,2,1,0:T(8,128)}) %all-reduce.4.cloned.1.call-update) | async-done | bytes 3735568
  283.7 1.9 fusion.10
  285.6 0.0 copy-done.2
  285.7 0.2 fusion.4
  285.9 0.0 copy-done.5
  285.9 0.3 fusion.5
  286.2 472.0 %all-to-all-done.1 = bf16[4,3584,2048]{1,2,0:T(8,128)(2,1)} async-done(((bf16[4,3584,2048]{1,2,0:T(8,128)(2,1)}), bf16[4,3584,2048]{1,2,0:T(8,128)(2,1)}, u32[]{:S(2)}, u32[]{:S(2)}) %all-to-all-start.1) | async-done | bytes 58720288 | tf_op jit(solution)/shard_map/all_to_all | solution.py:12
  758.2 0.0 copy-start.6
  758.2 0.0 copy-start.1
  758.2 25.0 %fusion.11 = f32[32,8192]{1,0:T(8,128)} fusion(bf16[32,3584]{1,0:T(8,128)(2,1)S(1)} %fusion.5, bf16[3584,8192]{0,1:T(8,128)(2,1)} %bitcast.7), kind=kOutput, calls=%fused_computation.15 | convolution fusion | flops 1879048192 | bytes 59998208 | tf_op jit(solution)/shard_map/dot_general | solution.py:67
  783.1 0.0 reduce-scatter.3.cloned.1.call-update
  783.2 0.0 copy-done.6
  783.2 0.6 dynamic-slice.2
  784.4 0.0 copy-done.1
  784.4 0.2 fusion.12
  784.7 20.3 %all-reduce.1 = f32[32,64]{1,0:T(8,128)S(1)} all-reduce(f32[32,64]{1,0:T(8,128)S(1)} %fusion.12), channel_id=4, replica_groups=mesh['groups'=2,'tensor'=4,'dp'=4] {'tensor'}, use_global_device_ids=true, to_apply=%region_2.3.clone | all-reduce | flops 2048 | bytes 16384
  804.9 6.9 reduce-scatter.3.cloned.1.call-done
  811.9 0.0 copy-done
  811.9 2.1 fusion.1
Async XLA Ops:
  6.5 805.3 %copy-start = (bf16[64,8192]{1,0:T(8,128)(2,1)S(1)}, bf16[64,8192]{1,0:T(8,128)(2,1)}, u32[]{:S(2)}) copy-start(bf16[64,8192]{1,0:T(8,128)(2,1)} %param.19) | copy-start | bytes 3145732
  6.5 23.1 %all-to-all-start = ((bf16[8,4,2048]{2,0,1:T(8,128)(2,1)}), bf16[8,4,2048]{2,0,1:T(8,128)(2,1)S(1)}, u32[]{:S(2)}, u32[]{:S(2)}) async-start(bf16[8,4,2048]{2,0,1:T(8,128)(2,1)} %bitcast.28), calls=%async_computation | async-start | bytes 262144 | tf_op jit(solution)/shard_map/all_to_all | solution.py:33
  53.1 12.7 %copy-start.3 = (bf16[2048,64]{0,1:T(8,128)(2,1)S(1)}, bf16[2048,64]{0,1:T(8,128)(2,1)}, u32[]{:S(2)}) copy-start(bf16[2048,64]{0,1:T(8,128)(2,1)} %param.14) | copy-start | bytes 786436
  53.1 13.0 %copy-start.4 = (bf16[2048,64]{0,1:T(8,128)(2,1)S(1)}, bf16[2048,64]{0,1:T(8,128)(2,1)}, u32[]{:S(2)}) copy-start(bf16[2048,64]{0,1:T(8,128)(2,1)} %param.16) | copy-start | bytes 786436
  53.1 705.1 %all-to-all-start.1 = ((bf16[4,3584,2048]{1,2,0:T(8,128)(2,1)}), bf16[4,3584,2048]{1,2,0:T(8,128)(2,1)}, u32[]{:S(2)}, u32[]{:S(2)}) async-start(bf16[4,3584,2048]{1,2,0:T(8,128)(2,1)} %stack.2), calls=%async_computation.1 | async-start | bytes 117440512 | tf_op jit(solution)/shard_map/all_to_all | solution.py:12
  65.7 218.0 %all-reduce.4.cloned.1.call-start = ((), (), s32[]{:S(2)}) async-start(), calls=%async_computation.4 | async-start | bytes 7471104
  110.8 32.6 %copy-start.7 = (u32[32]{0:T(128)S(1)}, u32[32]{0:T(128)}, u32[]{:S(2)}) copy-start(u32[32]{0:T(128)} %constant.9) | copy-start | bytes 388
  110.8 174.9 %copy-start.2 = (bf16[64,3584]{1,0:T(8,128)(2,1)S(1)}, bf16[64,3584]{1,0:T(8,128)(2,1)}, u32[]{:S(2)}) copy-start(bf16[64,3584]{1,0:T(8,128)(2,1)} %param.15) | copy-start | bytes 1376260
  110.8 175.1 %copy-start.5 = (bf16[64,3584]{1,0:T(8,128)(2,1)S(1)}, bf16[64,3584]{1,0:T(8,128)(2,1)}, u32[]{:S(2)}) copy-start(bf16[64,3584]{1,0:T(8,128)(2,1)} %param.17) | copy-start | bytes 1376260
  143.3 668.5 %reduce-scatter.3.cloned.1.call-start = ((), (), s32[]{:S(2)}) async-start(), calls=%async_computation.3 | async-start | bytes 1310720 | tf_op jit(solution)/shard_map/reduce_scatter | solution.py:72
  758.2 25.0 %copy-start.6 = (u32[32]{0:T(128)S(1)}, u32[32]{0:T(128)}, u32[]{:S(2)}) copy-start(u32[32]{0:T(128)} %constant.13) | copy-start | bytes 388
  758.2 26.2 %copy-start.1 = (bf16[3584,64]{0,1:T(8,128)(2,1)S(1)}, bf16[3584,64]{0,1:T(8,128)(2,1)}, u32[]{:S(2)}) copy-start(bf16[3584,64]{0,1:T(8,128)(2,1)} %param.18) | copy-start | bytes 1376260
Sparse Core Ops, SparseCore 0:
  143.4 140.2 all-reduce.3
  783.3 28.5 reduce-scatter.2
